TPU v7x, 32 devices: a whole 2x2x4 slice. The times are simulated.
32 devices in a mesh: groups: 2 (over x), tgt: 16 (over z, y, core).
Axes of the slice: x: 2, y: 2, z: 4, core: 2. Of those that a mesh axis runs over, the one named last changes fastest.
Arguments:
- source_feats: bfloat16 [4096, 1024], P(('groups', 'tgt')), parts along dimension 0, may hold values from -18 to 18
- target_feats: bfloat16 [16384, 1024], P(('groups', 'tgt')), parts along dimension 0, may hold values from -18 to 18
- source_logits: float32 [4096], P('groups'), parts along dimension 0, may hold values from -1.2 to 1.2
- target_logits: float32 [16384], P(('groups', 'tgt')), parts along dimension 0, may hold values from -1 to 3.4
Outputs:
- grad_source: float32 [4096, 1024], P(('groups', 'tgt')), parts along dimension 0
- grad_target: float32 [16384, 1024], P(('groups', 'tgt')), parts along dimension 0
- potential_src: float32 [4096], P('groups'), parts along dimension 0
- potential_tgt: float32 [16384], P(('groups', 'tgt')), parts along dimension 0
There are 2 independent parts, one for each index of `groups`. A program takes and returns all parts, laid end to end along the dimension named above; each array names one. Nothing has to cross between parts.
All inputs are finite; a program needn't handle non-finite values.
Results may differ from a plain program's by a relative error of at most 0.0033.
Values may be sent and summed in bfloat16 or wider, within the bound.
No kernel may reach another device: no remote copies, remote signals or barrier semaphores. Data moves between devices by JAX's collectives and lax.ppermute only.
A program may use at most 64 MiB of HBM per device.

v0:
```python
import math
import jax
import jax.numpy as jnp
from jax import lax
from jax.sharding import PartitionSpec as P

ITERS = 3


def per_device(source_feats, target_feats, source_logits, target_logits):
    width = target_feats.shape[1]
    scale = 1.0 / math.sqrt(width)
    source_count = source_feats.shape[0] * lax.axis_size("tgt")
    target_count = target_feats.shape[0] * lax.axis_size("tgt")
    log_source = source_logits - jnp.log(jnp.sum(jnp.exp(source_logits)))
    target_total = lax.psum(jnp.sum(jnp.exp(target_logits)), "tgt")
    log_target = target_logits - jnp.log(target_total)
    target_sq = jnp.sum(jnp.square(target_feats.astype(jnp.float32)), axis=1)
    gathered = lax.all_gather(source_feats, "tgt", axis=0, tiled=True)
    cross = lax.dot_general(
        gathered, target_feats, (((1,), (1,)), ((), ())), preferred_element_type=jnp.float32
    )
    gathered_sq = jnp.sum(jnp.square(gathered.astype(jnp.float32)), axis=1)
    cost = (gathered_sq[:, None] + target_sq[None, :] - 2.0 * cross) * scale
    potential_tgt = jnp.zeros((target_feats.shape[0],), jnp.float32)
    potential_src = jnp.zeros((source_count,), jnp.float32)
    for step in range(ITERS):
        scores = (log_target + potential_tgt)[None, :] - cost
        top = lax.pmax(jnp.max(scores, axis=1), "tgt")
        total = lax.psum(jnp.sum(jnp.exp(scores - top[:, None]), axis=1), "tgt")
        potential_src = -(top + jnp.log(total))
        column = (log_source + potential_src)[:, None] - cost
        column_top = jnp.max(column, axis=0)
        potential_tgt = -(
            column_top + jnp.log(jnp.sum(jnp.exp(column - column_top[None, :]), axis=0))
        )
    plan = jnp.exp(
        math.log(source_count)
        + (log_source + potential_src)[:, None]
        + (log_target + potential_tgt)[None, :]
        - cost
    ).astype(jnp.bfloat16)
    row_mass = jnp.sum(plan.astype(jnp.float32), axis=1)
    row_part = jnp.dot(plan, target_feats, preferred_element_type=jnp.float32)
    share_part, share_mass = (
        lax.psum_scatter(row_part, "tgt", scatter_dimension=0, tiled=True),
        lax.psum_scatter(row_mass, "tgt", scatter_dimension=0, tiled=True),
    )
    grad_source = share_mass[:, None] * source_feats.astype(jnp.float32) - share_part
    col_part = lax.dot_general(
        plan, gathered, (((0,), (0,)), ((), ())), preferred_element_type=jnp.float32
    )
    col_mass = jnp.sum(plan.astype(jnp.float32), axis=0)
    grad_target = (
        target_count
        / source_count
        * (col_mass[:, None] * target_feats.astype(jnp.float32) - col_part)
    )
    return (grad_source, grad_target, potential_src, potential_tgt)


def solution(mesh):
    return jax.shard_map(
        per_device,
        mesh=mesh,
        in_specs=(
            P(("groups", "tgt"), None),
            P(("groups", "tgt"), None),
            P("groups"),
            P(("groups", "tgt")),
        ),
        out_specs=(
            P(("groups", "tgt"), None),
            P(("groups", "tgt"), None),
            P("groups"),
            P(("groups", "tgt")),
        ),
        check_vma=False,
    )
```

profile of v0, /device:TPU:0, one launch (start us, length us, event | category | flops | bytes accessed | tf_op | source)
XLA Modules:
  0.0 395.1 jit_solution(12551948818565337685)
XLA Ops:
  7.2 0.0 copy-start.5
  7.2 0.0 all-gather.2.cloned.1.call-start
  7.2 0.7 all-gather.2.cloned.1.call-update
  7.9 0.0 reduce-scatter.2.cloned.1.call-start
  8.0 1.3 exponential_reduce_fusion.7
  9.3 36.0 %psum.28 = f32[]{:T(128)} all-reduce(f32[]{:T(128)} %exponential_reduce_fusion.7), channel_id=1, replica_groups=mesh['groups'=2,'tgt'=16] {'tgt'}, use_global_device_ids=true, to_apply=%region_2.0 | all-reduce | flops 1 | bytes 8 | tf_op jit(solution)/shard_map/psum | solution.py:16
  45.9 1.3 exponential_reduce_fusion.6
  47.9 1.5 fusion
  49.5 0.7 broadcast_subtract_fusion
  50.2 13.4 %all-gather.2.cloned.1.call-done = bf16[2048,1024]{1,0:T(8,128)(2,1)} async-done(((bf16[128,1024]{1,0:T(8,128)(2,1)}), bf16[2048,1024]{1,0:T(8,128)(2,1)}) %all-gather.2.cloned.1.call-update) | async-done | bytes 4194320 | tf_op jit(solution)/shard_map/all_gather | solution.py:19
  63.6 0.0 copy-start.3
  63.6 3.2 multiply_reduce_fusion
  66.8 0.0 copy-done.5
  66.8 0.2 copy-done.3
  67.0 4.8 %subtract_reduce_fusion.5 = (f32[2048]{0:T(1024)S(1)}, f32[2048,512]{1,0:T(8,128)}) fusion(f32[512]{0:T(512)S(1)} %broadcast_subtract_fusion, bf16[2048,1024]{1,0:T(8,128)(2,1)S(1)} %copy-done.3, bf16[512,1024]{1,0:T(8,128)(2,1)S(1)} %copy-done.5, f32[512]{0:T(512)S(1)} %fusion, f32[2048]{0:T(1024)S(1)} %multiply_reduce_fusion), kind=kOutput, calls=%fused_computation.16 | convolution fusion | flops 2153773056 | bytes 9457664 | tf_op jit(solution)/shard_map/dot_general | solution.py:20
  71.8 0.0 copy-start.6
  71.8 31.6 %pmax.21 = f32[2048]{0:T(1024)S(1)} all-reduce(f32[2048]{0:T(1024)S(1)} %get-tuple-element.12), channel_id=1, replica_groups=mesh['groups'=2,'tgt'=16] {'tgt'}, use_global_device_ids=true, to_apply=%region_6.0 | all-reduce | flops 2048 | bytes 16384 | tf_op jit(solution)/shard_map/pmax | solution.py:29
  103.5 3.2 exponential_reduce_fusion.5
  106.7 30.0 %psum.29 = f32[2048]{0:T(1024)S(1)} all-reduce(f32[2048]{0:T(1024)S(1)} %exponential_reduce_fusion.5), channel_id=1, replica_groups=mesh['groups'=2,'tgt'=16] {'tgt'}, use_global_device_ids=true, to_apply=%region_8.0 | all-reduce | flops 2048 | bytes 16384 | tf_op jit(solution)/shard_map/psum | solution.py:30
  136.7 0.0 copy-done.6
  136.7 0.0 copy-start
  136.7 0.0 copy-start.7
  136.8 2.7 subtract_reduce_fusion.4
  139.4 0.7 copy-done
  140.2 0.8 exponential_reduce_fusion.4
  140.9 0.0 copy-done.7
  141.0 0.4 subtract_reduce_fusion.3
  141.3 30.0 %pmax.22 = f32[2048]{0:T(1024)S(1)} all-reduce(f32[2048]{0:T(1024)S(1)} %subtract_reduce_fusion.3), channel_id=1, replica_groups=mesh['groups'=2,'tgt'=16] {'tgt'}, use_global_device_ids=true, to_apply=%region_12.0 | all-reduce | flops 2048 | bytes 16384 | tf_op jit(solution)/shard_map/pmax | solution.py:29
  171.3 3.2 exponential_reduce_fusion.3
  174.5 30.0 %psum.30 = f32[2048]{0:T(1024)S(1)} all-reduce(f32[2048]{0:T(1024)S(1)} %exponential_reduce_fusion.3), channel_id=1, replica_groups=mesh['groups'=2,'tgt'=16] {'tgt'}, use_global_device_ids=true, to_apply=%region_14.0 | all-reduce | flops 2048 | bytes 16384 | tf_op jit(solution)/shard_map/psum | solution.py:30
  204.5 0.0 copy-start.1
  204.6 2.7 subtract_reduce_fusion.2
  207.3 0.7 copy-done.1
  208.0 0.8 exponential_reduce_fusion.2
  208.8 0.4 subtract_reduce_fusion.1
  209.1 30.0 %pmax.23 = f32[2048]{0:T(1024)S(1)} all-reduce(f32[2048]{0:T(1024)S(1)} %subtract_reduce_fusion.1), channel_id=1, replica_groups=mesh['groups'=2,'tgt'=16] {'tgt'}, use_global_device_ids=true, to_apply=%region_18.0 | all-reduce | flops 2048 | bytes 16384 | tf_op jit(solution)/shard_map/pmax | solution.py:29
  239.1 3.2 exponential_reduce_fusion.1
  242.3 30.2 %psum.31 = f32[2048]{0:T(1024)S(1)} all-reduce(f32[2048]{0:T(1024)S(1)} %exponential_reduce_fusion.1), channel_id=1, replica_groups=mesh['groups'=2,'tgt'=16] {'tgt'}, use_global_device_ids=true, to_apply=%region_20.0 | all-reduce | flops 2048 | bytes 16384 | tf_op jit(solution)/shard_map/psum | solution.py:30
  272.5 0.0 copy-start.2
  272.5 0.6 broadcast_add_fusion
  273.1 2.9 subtract_reduce_fusion
  276.0 0.0 copy-done.2
  276.0 0.8 exponential_reduce_fusion
  276.8 0.6 fusion.3
  277.4 1.3 convert_reduce_fusion
  278.7 5.6 %fusion.4 = f32[2048,1024]{1,0:T(8,128)} fusion(bf16[2048,512]{1,0:T(8,128)(2,1)S(1)} %get-tuple-element.6, bf16[512,1024]{1,0:T(8,128)(2,1)S(1)} %copy-done.5), kind=kOutput, calls=%fused_computation.35 | convolution fusion | flops 2147483648 | bytes 11534336 | tf_op jit(solution)/shard_map/dot_general | solution.py:44
  284.3 0.0 copy-start.8
  284.3 0.0 reduce-scatter.2.cloned.1.call-update
  284.3 0.6 copy-done.8
  284.9 0.6 dynamic-slice
  286.2 30.1 %all-reduce = f32[2048]{0:T(1024)S(1)} all-reduce(f32[2048]{0:T(1024)S(1)} %get-tuple-element.5), channel_id=2, replica_groups=mesh['groups'=2,'tgt'=16] {'tgt'}, use_global_device_ids=true, to_apply=%region_24.0.clone | all-reduce | flops 2048 | bytes 16384
  316.3 0.1 dynamic-slice.1
  316.3 0.0 copy-start.4
  316.3 5.9 %fusion.2 = f32[512,1024]{1,0:T(8,128)} fusion(bf16[512,1024]{1,0:T(8,128)(2,1)S(1)} %copy-done.5, bf16[2048,512]{1,0:T(8,128)(2,1)S(1)} %get-tuple-element.6, bf16[2048,1024]{1,0:T(8,128)(2,1)} %all-gather.2.cloned.1.call-done, f32[512]{0:T(512)S(1)} %get-tuple-element.4), kind=kOutput, calls=%fused_computation.21 | convolution fusion | flops 2149580800 | bytes 9439232 | tf_op jit(solution)/shard_map/dot_general | solution.py:50
  322.2 64.0 %reduce-scatter.2.cloned.1.call-done = f32[128,1024]{1,0:T(8,128)} async-done(((f32[2048,1024]{1,0:T(8,128)}), f32[128,1024]{1,0:T(8,128)}) %reduce-scatter.2.cloned.1.call-update) | async-done | bytes 524304 | tf_op jit(solution)/shard_map/reduce_scatter | solution.py:46
  386.3 0.0 copy-done.4
  386.3 2.0 multiply_subtract_fusion
  (4 shorter events, 0.0 us)
Async XLA Ops:
  7.2 59.6 %copy-start.5 = (bf16[512,1024]{1,0:T(8,128)(2,1)S(1)}, bf16[512,1024]{1,0:T(8,128)(2,1)}, u32[]{:S(2)}) copy-start(bf16[512,1024]{1,0:T(8,128)(2,1)} %param.5) | copy-start | bytes 3145732
  7.2 56.4 %all-gather.2.cloned.1.call-start = ((), (), s32[]{:S(2)}) async-start(), calls=%async_computation.1 | async-start | bytes 4456448 | tf_op jit(solution)/shard_map/all_gather | solution.py:19
  7.9 378.4 %reduce-scatter.2.cloned.1.call-start = ((), (), s32[]{:S(2)}) async-start(), calls=%async_computation.2 | async-start | bytes 8912896 | tf_op jit(solution)/shard_map/reduce_scatter | solution.py:46
  63.6 3.4 copy-start.3
  71.8 64.9 %copy-start.6 = (f32[2048]{0:T(1024)S(1)}, f32[2048]{0:T(1024)}, u32[]{:S(2)}) copy-start(f32[2048]{0:T(1024)} %param.6) | copy-start | bytes 24580
  136.7 3.5 copy-start
  136.7 4.2 %copy-start.7 = (f32[512]{0:T(512)S(1)}, f32[512]{0:T(512)}, u32[]{:S(2)}) copy-start(f32[512]{0:T(512)} %param.7) | copy-start | bytes 6148
  204.5 3.5 copy-start.1
  272.5 3.5 copy-start.2
  284.3 0.7 copy-start.8
  316.3 69.9 %copy-start.4 = (bf16[128,1024]{1,0:T(8,128)(2,1)S(1)}, bf16[128,1024]{1,0:T(8,128)(2,1)}, u32[]{:S(2)}) copy-start(bf16[128,1024]{1,0:T(8,128)(2,1)} %param.4) | copy-start | bytes 786436
Sparse Core Ops, SparseCore 0:
  10.2 53.3 all-gather.1
  284.4 101.8 reduce-scatter.1
where the time goes:
time: 396 us; the launch traced here: 395 us
  blocking collectives  248 us (63%)
  waiting for transfers between devices  78.1 us (20%)
  other arithmetic  33.4 us (8%)
  matrix products  16.3 us (4%)
  between operations  16.3 us (4%)
    pmax x3, blocking collectives, per_device(): top = lax.pmax(jnp.max(scores, axis=1), 'tgt')  91.6 us
    psum x3, blocking collectives, per_device(): total = lax.psum(jnp.sum(jnp.exp(scores - top[:, None]), axis=1), 'tgt')  90.2 us
    reduce_scatter x1, waiting for transfers between devices, per_device(): lax.psum_scatter(row_part, 'tgt', scatter_dimension=0, tiled=True)  64 us
    psum x1, blocking collectives, per_device(): target_total = lax.psum(jnp.sum(jnp.exp(target_logits)), 'tgt')  36 us
    unnamed x1, blocking collectives  30.1 us
    all_gather x1, waiting for transfers between devices, per_device(): gathered = lax.all_gather(source_feats, 'tgt', axis=0, tiled=True)  13.4 us
    reduce_sum x3, other arithmetic, per_device(): total = lax.psum(jnp.sum(jnp.exp(scores - top[:, None]), axis=1), 'tgt')  9.62 us
    reduce_max x3, other arithmetic, per_device(): column_top = jnp.max(column, axis=0)  8.23 us
  transfers between devices with their start and end apart: 2, of which 2 were waited for; matrix products, arithmetic and copies ran while one was open for 3% of the time, Pallas kernels for 0%

commit v1 on v0

--- a/solution.py
+++ b/solution.py
@@ -5,6 +5,28 @@
 from jax.sharding import PartitionSpec as P
 
 ITERS = 3
+
+
+def in_order(tiles, dim):
+    lengths = list(tiles.shape[1:])
+    lengths[dim] *= tiles.shape[0]
+    return jnp.moveaxis(tiles, 0, dim).reshape(lengths)
+
+
+def gather_around(shard, axis, dim):
+    count = lax.axis_size(axis)
+    pairs = [(i, (i + 1) % count) for i in range(count)]
+    back = [(b, a) for a, b in pairs]
+    lower, upper = ([], [])
+    for lap in range(count - 1):
+        if lap % 2 == 0:
+            lower.append(lax.ppermute(lower[-1] if lower else shard, axis, pairs))
+        else:
+            upper.append(lax.ppermute(upper[-1] if upper else shard, axis, back))
+    blocks = jnp.stack([*lower[::-1], shard, *upper])
+    shift = lax.axis_index(axis) - len(lower)
+    blocks = blocks[(jnp.arange(count) - shift) % count]
+    return in_order(blocks, dim)
 
 
 def per_device(source_feats, target_feats, source_logits, target_logits):
@@ -16,7 +38,7 @@
     target_total = lax.psum(jnp.sum(jnp.exp(target_logits)), "tgt")
     log_target = target_logits - jnp.log(target_total)
     target_sq = jnp.sum(jnp.square(target_feats.astype(jnp.float32)), axis=1)
-    gathered = lax.all_gather(source_feats, "tgt", axis=0, tiled=True)
+    gathered = gather_around(source_feats, "tgt", 0)
     cross = lax.dot_general(
         gathered, target_feats, (((1,), (1,)), ((), ())), preferred_element_type=jnp.float32
     )

time: 396 us -> 455 us (1.15)
  starting transfers between devices: 0.08 us -> 28.2 us
  local copies, waits for them, and re-layouts: 2.98 us -> 21.6 us
  waiting for transfers between devices: 78.1 us -> 93.6 us
    ppermute x0 -> x15, waiting for transfers between devices: none -> 29 us  [the longest x8 27.9 us: gather_around(): lower.append(lax.ppermute(lower[-1] if lower else shard, axis, pairs))]
    ppermute x0 -> x15, starting transfers between devices: none -> 28.1 us  [the longest x7 27.6 us: gather_around(): upper.append(lax.ppermute(upper[-1] if upper else shard, axis, back))]
    all_gather x1 -> x0, waiting for transfers between devices: 13.4 us -> none  [per_device(): gathered = lax.all_gather(source_feats, 'tgt', axis=0, tiled=True)]
    unnamed x20 -> x35, local copies, waits for them, and re-layouts: 2.98 us -> 15.8 us
    gather x0 -> x1, local copies, waits for them, and re-layouts: none -> 5.06 us  [gather_around(): blocks = blocks[(jnp.arange(count) - shift) % count]]
  transfers between devices with their start and end apart: 2 -> 16, of which waited for: 2 -> 10; matrix products, arithmetic and copies ran while one was open for 3% -> 5% of each run, Pallas kernels for 0% -> 0%
where the time goes in v1:
time: 455 us
  blocking collectives  245 us (54%)
  waiting for transfers between devices  93.6 us (21%)
  other arithmetic  33.4 us (7%)
  starting transfers between devices  28.2 us (6%)
  local copies, waits for them, and re-layouts  21.6 us (5%)
  between operations  16.3 us (4%)
  matrix products  16.2 us (4%)
    pmax x3, blocking collectives, per_device(): top = lax.pmax(jnp.max(scores, axis=1), 'tgt')  90.5 us
    psum x3, blocking collectives, per_device(): total = lax.psum(jnp.sum(jnp.exp(scores - top[:, None]), axis=1), 'tgt')  90.2 us
    reduce_scatter x1, waiting for transfers between devices, per_device(): lax.psum_scatter(row_part, 'tgt', scatter_dimension=0, tiled=True)  64.6 us
    psum x1, blocking collectives, per_device(): target_total = lax.psum(jnp.sum(jnp.exp(target_logits)), 'tgt')  34.5 us
    unnamed x1, blocking collectives  30.1 us
    ppermute x8, waiting for transfers between devices, gather_around(): lower.append(lax.ppermute(lower[-1] if lower else shard, axis, pairs))  27.9 us
    ppermute x7, starting transfers between devices, gather_around(): upper.append(lax.ppermute(upper[-1] if upper else shard, axis, back))  27.6 us
    unnamed x35, local copies, waits for them, and re-layouts  15.8 us
  transfers between devices with their start and end apart: 16, of which 10 were waited for; matrix products, arithmetic and copies ran while one was open for 5% of the time, Pallas kernels for 0%

profile of v1, /device:TPU:0, one launch (start us, length us, event | category | flops | bytes accessed | tf_op | source)
XLA Modules:
  0.0 454.6 jit_solution(8366816049143162161)
XLA Ops:
  7.7 9.3 %collective-permute-done = bf16[128,1024]{1,0:T(8,128)(2,1)S(1)} collective-permute-done((bf16[128,1024]{1,0:T(8,128)(2,1)}, bf16[128,1024]{1,0:T(8,128)(2,1)S(1)}, u32[]{:S(2)}, u32[]{:S(2)}) %collective-permute-start) | collective-permute-done | bytes 262176 | tf_op jit(solution)/shard_map/ppermute | solution.py:23
  17.0 4.4 collective-permute-start.8
  21.4 4.1 collective-permute-done.1
  25.6 4.6 %collective-permute-start.9 = (bf16[128,1024]{1,0:T(8,128)(2,1)S(1)}, bf16[128,1024]{1,0:T(8,128)(2,1)S(1)}, u32[]{:S(2)}, u32[]{:S(2)}) collective-permute-start(bf16[128,1024]{1,0:T(8,128)(2,1)S(1)} %collective-permute-done.8), channel_id=1, source_target_pairs={{1,0},{2,1},{3,2},{4,3},{5,4},{6,5},{7,6},{8,7},{9,8},{10,9},{11,1... | collective-permute-start | bytes 786440 | tf_op jit(solution)/shard_map/ppermute | solution.py:25
  30.2 3.8 collective-permute-done.2
  34.1 4.7 %collective-permute-start.10 = (bf16[128,1024]{1,0:T(8,128)(2,1)S(1)}, bf16[128,1024]{1,0:T(8,128)(2,1)S(1)}, u32[]{:S(2)}, u32[]{:S(2)}) collective-permute-start(bf16[128,1024]{1,0:T(8,128)(2,1)S(1)} %collective-permute-done.9), channel_id=1, source_target_pairs={{1,0},{2,1},{3,2},{4,3},{5,4},{6,5},{7,6},{8,7},{9,8},{10,9},{11,1... | collective-permute-start | bytes 786440 | tf_op jit(solution)/shard_map/ppermute | solution.py:25
  38.8 3.8 collective-permute-done.3
  42.7 4.7 %collective-permute-start.11 = (bf16[128,1024]{1,0:T(8,128)(2,1)S(1)}, bf16[128,1024]{1,0:T(8,128)(2,1)S(1)}, u32[]{:S(2)}, u32[]{:S(2)}) collective-permute-start(bf16[128,1024]{1,0:T(8,128)(2,1)S(1)} %collective-permute-done.10), channel_id=1, source_target_pairs={{1,0},{2,1},{3,2},{4,3},{5,4},{6,5},{7,6},{8,7},{9,8},{10,9},{11,1... | collective-permute-start | bytes 786440 | tf_op jit(solution)/shard_map/ppermute | solution.py:25
  47.4 3.8 collective-permute-done.4
  51.3 1.3 exponential_reduce_fusion.7
  52.6 1.3 exponential_reduce_fusion.6
  53.9 4.4 collective-permute-start.12
  58.3 1.5 collective-permute-done.5
  59.9 1.5 fusion
  61.4 0.9 collective-permute-done.12
  62.2 4.7 %collective-permute-start.13 = (bf16[128,1024]{1,0:T(8,128)(2,1)S(1)}, bf16[128,1024]{1,0:T(8,128)(2,1)S(1)}, u32[]{:S(2)}, u32[]{:S(2)}) collective-permute-start(bf16[128,1024]{1,0:T(8,128)(2,1)S(1)} %collective-permute-done.12), channel_id=1, source_target_pairs={{1,0},{2,1},{3,2},{4,3},{5,4},{6,5},{7,6},{8,7},{9,8},{10,9},{11,1... | collective-permute-start | bytes 786440 | tf_op jit(solution)/shard_map/ppermute | solution.py:25
  66.9 1.6 collective-permute-done.6
  68.5 34.5 %psum.28 = f32[]{:T(128)} all-reduce(f32[]{:T(128)} %exponential_reduce_fusion.7), channel_id=1, replica_groups=mesh['groups'=2,'tgt'=16] {'tgt'}, use_global_device_ids=true, to_apply=%region_2.0 | all-reduce | flops 1 | bytes 8 | tf_op jit(solution)/shard_map/psum | solution.py:38
  104.4 0.7 broadcast_subtract_fusion
  105.1 1.7 bitcast_dynamic-update-slice_fusion.15
  106.8 1.7 bitcast_dynamic-update-slice_fusion.14
  108.4 0.7 bitcast_dynamic-update-slice_fusion.13
  109.2 0.7 bitcast_dynamic-update-slice_fusion.12
  109.9 0.7 bitcast_dynamic-update-slice_fusion.11
  110.6 0.7 bitcast_dynamic-update-slice_fusion.10
  111.4 0.7 bitcast_dynamic-update-slice_fusion.9
  112.1 0.7 bitcast_dynamic-update-slice_fusion.8
  112.8 0.7 bitcast_dynamic-update-slice_fusion.7
  113.6 0.7 bitcast_dynamic-update-slice_fusion.6
  114.3 0.7 bitcast_dynamic-update-slice_fusion.5
  115.0 0.7 bitcast_dynamic-update-slice_fusion.4
  115.7 0.7 bitcast_dynamic-update-slice_fusion.3
  116.5 0.7 bitcast_dynamic-update-slice_fusion.2
  117.2 0.7 bitcast_dynamic-update-slice_fusion.1
  117.9 0.7 bitcast_dynamic-update-slice_fusion
  118.6 5.1 %gather_fusion = bf16[16,128,1024]{2,1,0:T(8,128)(2,1)} fusion(bf16[16,128,1024]{2,1,0:T(8,128)(2,1)} %bitcast_dynamic-update-slice_fusion, s32[1024]{0:T(1024)S(1)} %pad_clamp_fusion), kind=kCustom, calls=%fused_computation | custom fusion | bytes 8388672 | tf_op jit(solution)/shard_map/gather | solution.py:28
  123.7 3.2 multiply_reduce_fusion
  127.2 4.8 %subtract_reduce_fusion.5 = (f32[2048]{0:T(1024)S(1)}, f32[2048,512]{1,0:T(8,128)}) fusion(f32[512]{0:T(512)S(1)} %broadcast_subtract_fusion, bf16[2048,1024]{1,0:T(8,128)(2,1)S(1)} %bitcast.44, bf16[512,1024]{1,0:T(8,128)(2,1)S(1)} %copy-done.5, f32[512]{0:T(512)S(1)} %fusion, f32[2048]{0:T(1024)S(1)} %bitcast.45), kind=kOutput, calls=%fused_computation.17 | convolution fusion | flops 2153773056 | bytes 9457664 | tf_op jit(solution)/shard_map/dot_general | solution.py:42
  132.0 30.5 %pmax.21 = f32[2048]{0:T(1024)S(1)} all-reduce(f32[2048]{0:T(1024)S(1)} %get-tuple-element.12), channel_id=1, replica_groups=mesh['groups'=2,'tgt'=16] {'tgt'}, use_global_device_ids=true, to_apply=%region_6.7 | all-reduce | flops 2048 | bytes 16384 | tf_op jit(solution)/shard_map/pmax | solution.py:51
  162.5 3.2 exponential_reduce_fusion.5
  165.7 30.0 %psum.29 = f32[2048]{0:T(1024)S(1)} all-reduce(f32[2048]{0:T(1024)S(1)} %exponential_reduce_fusion.5), channel_id=1, replica_groups=mesh['groups'=2,'tgt'=16] {'tgt'}, use_global_device_ids=true, to_apply=%region_8.9 | all-reduce | flops 2048 | bytes 16384 | tf_op jit(solution)/shard_map/psum | solution.py:52
  195.7 2.7 subtract_reduce_fusion.4
  198.4 0.7 copy-done
  199.1 0.8 exponential_reduce_fusion.4
  200.3 30.0 %pmax.22 = f32[2048]{0:T(1024)S(1)} all-reduce(f32[2048]{0:T(1024)S(1)} %subtract_reduce_fusion.3), channel_id=1, replica_groups=mesh['groups'=2,'tgt'=16] {'tgt'}, use_global_device_ids=true, to_apply=%region_12.13 | all-reduce | flops 2048 | bytes 16384 | tf_op jit(solution)/shard_map/pmax | solution.py:51
  230.3 3.2 exponential_reduce_fusion.3
  233.5 30.2 %psum.30 = f32[2048]{0:T(1024)S(1)} all-reduce(f32[2048]{0:T(1024)S(1)} %exponential_reduce_fusion.3), channel_id=1, replica_groups=mesh['groups'=2,'tgt'=16] {'tgt'}, use_global_device_ids=true, to_apply=%region_14.15 | all-reduce | flops 2048 | bytes 16384 | tf_op jit(solution)/shard_map/psum | solution.py:52
  263.7 2.7 subtract_reduce_fusion.2
  266.4 0.7 copy-done.1
  267.1 0.8 exponential_reduce_fusion.2
  268.3 30.0 %pmax.23 = f32[2048]{0:T(1024)S(1)} all-reduce(f32[2048]{0:T(1024)S(1)} %subtract_reduce_fusion.1), channel_id=1, replica_groups=mesh['groups'=2,'tgt'=16] {'tgt'}, use_global_device_ids=true, to_apply=%region_18.19 | all-reduce | flops 2048 | bytes 16384 | tf_op jit(solution)/shard_map/pmax | solution.py:51
  298.3 3.2 exponential_reduce_fusion.1
  301.5 30.0 %psum.31 = f32[2048]{0:T(1024)S(1)} all-reduce(f32[2048]{0:T(1024)S(1)} %exponential_reduce_fusion.1), channel_id=1, replica_groups=mesh['groups'=2,'tgt'=16] {'tgt'}, use_global_device_ids=true, to_apply=%region_20.21 | all-reduce | flops 2048 | bytes 16384 | tf_op jit(solution)/shard_map/psum | solution.py:52
  331.5 0.6 broadcast_add_fusion
  332.1 2.9 subtract_reduce_fusion
  335.0 0.8 exponential_reduce_fusion
  335.7 0.6 fusion.5
  336.3 1.3 convert_reduce_fusion
  337.7 5.6 %fusion.6 = f32[2048,1024]{1,0:T(8,128)} fusion(bf16[2048,512]{1,0:T(8,128)(2,1)S(1)} %get-tuple-element.6, bf16[512,1024]{1,0:T(8,128)(2,1)S(1)} %copy-done.5), kind=kOutput, calls=%fused_computation.59 | convolution fusion | flops 2147483648 | bytes 11534336 | tf_op jit(solution)/shard_map/dot_general | solution.py:66
  343.3 0.6 copy-done.8
  345.1 30.1 %all-reduce = f32[2048]{0:T(1024)S(1)} all-reduce(f32[2048]{0:T(1024)S(1)} %get-tuple-element.5), channel_id=2, replica_groups=mesh['groups'=2,'tgt'=16] {'tgt'}, use_global_device_ids=true, to_apply=%region_24.25.clone | all-reduce | flops 2048 | bytes 16384
  375.3 5.9 %fusion.2 = f32[512,1024]{1,0:T(8,128)} fusion(bf16[512,1024]{1,0:T(8,128)(2,1)S(1)} %copy-done.5, bf16[2048,512]{1,0:T(8,128)(2,1)S(1)} %get-tuple-element.6, bf16[2048,1024]{1,0:T(8,128)(2,1)} %bitcast.43, f32[512]{0:T(512)S(1)} %get-tuple-element.4), kind=kOutput, calls=%fused_computation.22 | convolution fusion | flops 2149580800 | bytes 9439232 | tf_op jit(solution)/shard_map/dot_general | solution.py:72
  381.2 64.6 %reduce-scatter.2.cloned.1.call-done = f32[128,1024]{1,0:T(8,128)} async-done(((f32[2048,1024]{1,0:T(8,128)}), f32[128,1024]{1,0:T(8,128)}) %reduce-scatter.2.cloned.1.call-update) | async-done | bytes 524304 | tf_op jit(solution)/shard_map/reduce_scatter | solution.py:68
  445.8 2.0 multiply_subtract_fusion
  (43 shorter events, 2.5 us)
Async XLA Ops:
  7.2 105.6 %copy-start.4 = (bf16[128,1024]{1,0:T(8,128)(2,1)S(1)}, bf16[128,1024]{1,0:T(8,128)(2,1)}, u32[]{:S(2)}) copy-start(bf16[128,1024]{1,0:T(8,128)(2,1)} %param.4) | copy-start | bytes 786436
  7.2 438.6 %reduce-scatter.2.cloned.1.call-start = ((), (), s32[]{:S(2)}) async-start(), calls=%async_computation.1 | async-start | bytes 8912896 | tf_op jit(solution)/shard_map/reduce_scatter | solution.py:68
  7.2 9.8 %collective-permute-start = (bf16[128,1024]{1,0:T(8,128)(2,1)}, bf16[128,1024]{1,0:T(8,128)(2,1)S(1)}, u32[]{:S(2)}, u32[]{:S(2)}) collective-permute-start(bf16[128,1024]{1,0:T(8,128)(2,1)} %param.4), channel_id=1, source_target_pairs={{0,1},{1,2},{2,3},{3,4},{4,5},{5,6},{6,7},{7,8},{8,9},{9,10},{10,1... | collective-permute-start | bytes 786440 | tf_op jit(solution)/shard_map/ppermute | solution.py:23
  17.0 8.5 %collective-permute-start.1 = (bf16[128,1024]{1,0:T(8,128)(2,1)S(1)}, bf16[128,1024]{1,0:T(8,128)(2,1)S(1)}, u32[]{:S(2)}, u32[]{:S(2)}) collective-permute-start(bf16[128,1024]{1,0:T(8,128)(2,1)S(1)} %collective-permute-done), channel_id=1, source_target_pairs={{0,1},{1,2},{2,3},{3,4},{4,5},{5,6},{6,7},{7,8},{8,9},{9,10},{10,1... | collective-permute-start | bytes 786440 | tf_op jit(solution)/shard_map/ppermute | solution.py:23
  17.0 8.6 %collective-permute-start.8 = (bf16[128,1024]{1,0:T(8,128)(2,1)}, bf16[128,1024]{1,0:T(8,128)(2,1)S(1)}, u32[]{:S(2)}, u32[]{:S(2)}) collective-permute-start(bf16[128,1024]{1,0:T(8,128)(2,1)} %param.4), channel_id=1, source_target_pairs={{1,0},{2,1},{3,2},{4,3},{5,4},{6,5},{7,6},{8,7},{9,8},{10,9},{11,1... | collective-permute-start | bytes 786440 | tf_op jit(solution)/shard_map/ppermute | solution.py:25
  25.5 8.6 %collective-permute-start.2 = (bf16[128,1024]{1,0:T(8,128)(2,1)S(1)}, bf16[128,1024]{1,0:T(8,128)(2,1)S(1)}, u32[]{:S(2)}, u32[]{:S(2)}) collective-permute-start(bf16[128,1024]{1,0:T(8,128)(2,1)S(1)} %collective-permute-done.1), channel_id=1, source_target_pairs={{0,1},{1,2},{2,3},{3,4},{4,5},{5,6},{6,7},{7,8},{8,9},{9,10},{10,1... | collective-permute-start | bytes 786440 | tf_op jit(solution)/shard_map/ppermute | solution.py:23
  25.6 8.5 %collective-permute-start.9 = (bf16[128,1024]{1,0:T(8,128)(2,1)S(1)}, bf16[128,1024]{1,0:T(8,128)(2,1)S(1)}, u32[]{:S(2)}, u32[]{:S(2)}) collective-permute-start(bf16[128,1024]{1,0:T(8,128)(2,1)S(1)} %collective-permute-done.8), channel_id=1, source_target_pairs={{1,0},{2,1},{3,2},{4,3},{5,4},{6,5},{7,6},{8,7},{9,8},{10,9},{11,1... | collective-permute-start | bytes 786440 | tf_op jit(solution)/shard_map/ppermute | solution.py:25
  34.1 8.6 %collective-permute-start.3 = (bf16[128,1024]{1,0:T(8,128)(2,1)S(1)}, bf16[128,1024]{1,0:T(8,128)(2,1)S(1)}, u32[]{:S(2)}, u32[]{:S(2)}) collective-permute-start(bf16[128,1024]{1,0:T(8,128)(2,1)S(1)} %collective-permute-done.2), channel_id=1, source_target_pairs={{0,1},{1,2},{2,3},{3,4},{4,5},{5,6},{6,7},{7,8},{8,9},{9,10},{10,1... | collective-permute-start | bytes 786440 | tf_op jit(solution)/shard_map/ppermute | solution.py:23
  34.1 8.6 %collective-permute-start.10 = (bf16[128,1024]{1,0:T(8,128)(2,1)S(1)}, bf16[128,1024]{1,0:T(8,128)(2,1)S(1)}, u32[]{:S(2)}, u32[]{:S(2)}) collective-permute-start(bf16[128,1024]{1,0:T(8,128)(2,1)S(1)} %collective-permute-done.9), channel_id=1, source_target_pairs={{1,0},{2,1},{3,2},{4,3},{5,4},{6,5},{7,6},{8,7},{9,8},{10,9},{11,1... | collective-permute-start | bytes 786440 | tf_op jit(solution)/shard_map/ppermute | solution.py:25
  42.7 8.6 %collective-permute-start.4 = (bf16[128,1024]{1,0:T(8,128)(2,1)S(1)}, bf16[128,1024]{1,0:T(8,128)(2,1)S(1)}, u32[]{:S(2)}, u32[]{:S(2)}) collective-permute-start(bf16[128,1024]{1,0:T(8,128)(2,1)S(1)} %collective-permute-done.3), channel_id=1, source_target_pairs={{0,1},{1,2},{2,3},{3,4},{4,5},{5,6},{6,7},{7,8},{8,9},{9,10},{10,1... | collective-permute-start | bytes 786440 | tf_op jit(solution)/shard_map/ppermute | solution.py:23
  42.7 11.2 %collective-permute-start.11 = (bf16[128,1024]{1,0:T(8,128)(2,1)S(1)}, bf16[128,1024]{1,0:T(8,128)(2,1)S(1)}, u32[]{:S(2)}, u32[]{:S(2)}) collective-permute-start(bf16[128,1024]{1,0:T(8,128)(2,1)S(1)} %collective-permute-done.10), channel_id=1, source_target_pairs={{1,0},{2,1},{3,2},{4,3},{5,4},{6,5},{7,6},{8,7},{9,8},{10,9},{11,1... | collective-permute-start | bytes 786440 | tf_op jit(solution)/shard_map/ppermute | solution.py:25
  51.3 8.6 %collective-permute-start.5 = (bf16[128,1024]{1,0:T(8,128)(2,1)S(1)}, bf16[128,1024]{1,0:T(8,128)(2,1)S(1)}, u32[]{:S(2)}, u32[]{:S(2)}) collective-permute-start(bf16[128,1024]{1,0:T(8,128)(2,1)S(1)} %collective-permute-done.4), channel_id=1, source_target_pairs={{0,1},{1,2},{2,3},{3,4},{4,5},{5,6},{6,7},{7,8},{8,9},{9,10},{10,1... | collective-permute-start | bytes 786440 | tf_op jit(solution)/shard_map/ppermute | solution.py:23
  53.9 8.3 %collective-permute-start.12 = (bf16[128,1024]{1,0:T(8,128)(2,1)S(1)}, bf16[128,1024]{1,0:T(8,128)(2,1)S(1)}, u32[]{:S(2)}, u32[]{:S(2)}) collective-permute-start(bf16[128,1024]{1,0:T(8,128)(2,1)S(1)} %collective-permute-done.11), channel_id=1, source_target_pairs={{1,0},{2,1},{3,2},{4,3},{5,4},{6,5},{7,6},{8,7},{9,8},{10,9},{11,1... | collective-permute-start | bytes 786440 | tf_op jit(solution)/shard_map/ppermute | solution.py:25
  59.8 8.6 %collective-permute-start.6 = (bf16[128,1024]{1,0:T(8,128)(2,1)S(1)}, bf16[128,1024]{1,0:T(8,128)(2,1)}, u32[]{:S(2)}, u32[]{:S(2)}) collective-permute-start(bf16[128,1024]{1,0:T(8,128)(2,1)S(1)} %collective-permute-done.5), channel_id=1, source_target_pairs={{0,1},{1,2},{2,3},{3,4},{4,5},{5,6},{6,7},{7,8},{8,9},{9,10},{10,1... | collective-permute-start | bytes 786440 | tf_op jit(solution)/shard_map/ppermute | solution.py:23
  62.2 42.9 %collective-permute-start.13 = (bf16[128,1024]{1,0:T(8,128)(2,1)S(1)}, bf16[128,1024]{1,0:T(8,128)(2,1)S(1)}, u32[]{:S(2)}, u32[]{:S(2)}) collective-permute-start(bf16[128,1024]{1,0:T(8,128)(2,1)S(1)} %collective-permute-done.12), channel_id=1, source_target_pairs={{1,0},{2,1},{3,2},{4,3},{5,4},{6,5},{7,6},{8,7},{9,8},{10,9},{11,1... | collective-permute-start | bytes 786440 | tf_op jit(solution)/shard_map/ppermute | solution.py:25
  68.5 36.6 %collective-permute-start.7 = (bf16[128,1024]{1,0:T(8,128)(2,1)}, bf16[128,1024]{1,0:T(8,128)(2,1)}, u32[]{:S(2)}, u32[]{:S(2)}) collective-permute-start(bf16[128,1024]{1,0:T(8,128)(2,1)} %collective-permute-done.6), channel_id=1, source_target_pairs={{0,1},{1,2},{2,3},{3,4},{4,5},{5,6},{6,7},{7,8},{8,9},{9,10},{10,1... | collective-permute-start | bytes 786440 | tf_op jit(solution)/shard_map/ppermute | solution.py:23
  105.1 12.8 %collective-permute-start.14 = (bf16[128,1024]{1,0:T(8,128)(2,1)S(1)}, bf16[128,1024]{1,0:T(8,128)(2,1)S(1)}, u32[]{:S(2)}, u32[]{:S(2)}) collective-permute-start(bf16[128,1024]{1,0:T(8,128)(2,1)S(1)} %collective-permute-done.13), channel_id=1, source_target_pairs={{1,0},{2,1},{3,2},{4,3},{5,4},{6,5},{7,6},{8,7},{9,8},{10,9},{11,1... | collective-permute-start | bytes 786440 | tf_op jit(solution)/shard_map/ppermute | solution.py:25
  118.6 8.3 %copy-start.5 = (bf16[512,1024]{1,0:T(8,128)(2,1)S(1)}, bf16[512,1024]{1,0:T(8,128)(2,1)}, u32[]{:S(2)}) copy-start(bf16[512,1024]{1,0:T(8,128)(2,1)} %param.5) | copy-start | bytes 3145732
  123.7 3.4 copy-start.3
  132.0 63.7 %copy-start.6 = (f32[2048]{0:T(1024)S(1)}, f32[2048]{0:T(1024)}, u32[]{:S(2)}) copy-start(f32[2048]{0:T(1024)} %param.6) | copy-start | bytes 24580
  195.7 3.5 copy-start
  195.7 4.2 copy-start.7
  263.7 3.5 copy-start.1
  331.5 3.5 copy-start.2
  343.2 0.7 copy-start.8
Sparse Core Ops, SparseCore 0:
  343.4 102.3 reduce-scatter.1
